TPU v7x, 32 devices: a whole 2x2x4 slice. The times are simulated.
32 devices in a mesh: row: 4 (over y, x), col: 8 (over z, core).
Axes of the slice: x: 2, y: 2, z: 4, core: 2. Of those that a mesh axis runs over, the one named last changes fastest.
Arguments:
- momentum: float32 [4608, 8192], P('row', 'col'), may hold values from -37 to 37
Outputs:
- update: float32 [4608, 8192], P('row', 'col')
All inputs are finite; a program needn't handle non-finite values.
Results may differ from a plain program's by a relative error of at most 0.0049.
Values may be sent and summed in bfloat16 or wider, within the bound.
No kernel may reach another device: no remote copies, remote signals or barrier semaphores. Data moves between devices by JAX's collectives and lax.ppermute only.
A program may use at most 128 MiB of HBM per device.

v0:
```python
import math
import jax
import jax.numpy as jnp
from jax import lax
from jax.sharding import PartitionSpec as P

ROWS = 4608
COLS = 8192
quintic_a = 3.4445
quintic_b = -4.775
quintic_c = 2.0315


def from_root(shard, axis, root):
    mine = lax.axis_index(axis) == root
    return lax.psum(jnp.where(mine, shard, jnp.zeros_like(shard)), axis)


def rows_product(left, right):
    return lax.dot_general(
        left, right, (((1,), (1,)), ((), ())), preferred_element_type=jnp.float32
    )


def body(momentum):
    partial_sum = jnp.sum(momentum * momentum)
    norm_squares = lax.psum(partial_sum, ("row", "col"))
    factor = 0.6 * math.sqrt(ROWS) / (jnp.sqrt(norm_squares) + 1e-07)
    scaled = (momentum * factor).astype(jnp.bfloat16)
    tile_ratio = lax.axis_size("col") // lax.axis_size("row")
    col_index = lax.axis_index("col")
    source_row = col_index // tile_ratio
    half_index = col_index % tile_ratio
    row_panel = lax.all_gather(scaled, "col", axis=1, tiled=True)
    part_rows = row_panel.shape[0] // tile_ratio
    own_part = lax.dynamic_slice_in_dim(row_panel, half_index * part_rows, part_rows, 0)
    peer_rows = from_root(own_part, "row", source_row)
    gram = rows_product(row_panel, peer_rows).astype(jnp.bfloat16)
    gram_panel = lax.all_gather(gram, "col", axis=1, tiled=True)
    gram_columns = lax.all_gather(gram, "row", axis=0, tiled=True)
    squared = jnp.dot(gram_panel, gram_columns, preferred_element_type=jnp.float32)
    poly = (quintic_b * gram.astype(jnp.float32) + quintic_c * squared).astype(jnp.bfloat16)
    poly_panel = lax.all_gather(poly, "col", axis=1, tiled=True)
    product = jnp.dot(
        poly_panel,
        lax.all_gather(scaled, "row", axis=0, tiled=True),
        preferred_element_type=jnp.float32,
    )
    return math.sqrt(COLS) * (quintic_a * scaled.astype(jnp.float32) + product)


def solution(mesh):
    placed = (P("row", "col"),)
    return jax.shard_map(
        body, mesh=mesh, in_specs=placed, out_specs=P("row", "col"), check_vma=False
    )
```

profile of v0, /device:TPU:0, one launch (start us, length us, event | category | flops | bytes accessed | tf_op | source)
XLA Modules:
  0.0 828.4 jit_solution(4937114119938713192)
XLA Ops:
  6.5 0.0 all-gather.6.cloned.1.call-start
  6.5 4.2 multiply_reduce_fusion
  10.7 42.2 %psum.14 = f32[]{:T(128)} all-reduce(f32[]{:T(128)} %multiply_reduce_fusion), channel_id=1, replica_groups=mesh['row'=4,'col'=8] {'row','col'}, use_global_device_ids=true, to_apply=%region_1.0 | all-reduce | flops 1 | bytes 8 | tf_op jit(solution)/shard_map/psum | solution.py:27
  53.6 4.4 multiply_convert_fusion
  58.0 0.0 all-gather.6.cloned.1.call-update
  58.0 0.0 all-reduce.2.cloned.1.call-start
  58.1 168.3 %all-gather.6.cloned.1.call-done = bf16[1152,8192]{1,0:T(8,128)(2,1)} async-done(((bf16[1152,1024]{1,0:T(8,128)(2,1)}), bf16[1152,8192]{1,0:T(8,128)(2,1)}) %all-gather.6.cloned.1.call-update) | async-done | bytes 18874384 | tf_op jit(solution)/shard_map/all_gather | solution.py:34
  226.5 9.8 %dynamic-slice_select_fusion = bf16[576,8192]{1,0:T(8,128)(2,1)} fusion(bf16[1152,8192]{1,0:T(8,128)(2,1)} %all-gather.6.cloned.1.call-done, s32[]{:T(128)S(6)} %select_n.25, pred[]{:T(512)S(6)} %eq.5), kind=kLoop, calls=%fused_computation | loop fusion | flops 4718592 | bytes 18874372 | tf_op jit(solution)/shard_map/jit(_where)/select_n | solution.py:16
  236.2 0.0 all-reduce.2.cloned.1.call-update
  236.2 0.0 all-gather.10.cloned.1.call-start
  236.3 186.7 %all-reduce.2.cloned.1.call-done = bf16[576,8192]{1,0:T(8,128)(2,1)} async-done(((bf16[576,8192]{1,0:T(8,128)(2,1)}), bf16[576,8192]{1,0:T(8,128)(2,1)}) %all-reduce.2.cloned.1.call-update) | async-done | bytes 9437200 | tf_op jit(solution)/shard_map/psum | solution.py:16
  423.0 18.8 %convolution_convert_fusion = bf16[1152,576]{0,1:T(8,128)(2,1)} fusion(bf16[1152,8192]{1,0:T(8,128)(2,1)} %all-gather.6.cloned.1.call-done, bf16[576,8192]{1,0:T(8,128)(2,1)} %all-reduce.2.cloned.1.call-done), kind=kOutput, calls=%fused_computation.7 | convolution fusion | flops 10872299520 | bytes 29638656 | tf_op jit(solution)/shard_map/dot_general | solution.py:20
  441.8 0.0 all-gather.10.cloned.1.call-update
  441.9 0.0 all-gather.8.cloned.1.call-start
  441.9 0.5 all-gather.8.cloned.1.call-update
  442.4 0.0 all-gather.14.cloned.1.call-start
  442.5 0.5 all-gather.14.cloned.1.call-update
  443.0 0.0 copy-start
  443.0 0.2 all-gather.12.cloned.1.call-start
  443.3 60.6 %all-gather.10.cloned.1.call-done = bf16[4608,576]{0,1:T(8,128)(2,1)} async-done(((bf16[1152,576]{0,1:T(8,128)(2,1)}), bf16[4608,576]{0,1:T(8,128)(2,1)}) %all-gather.10.cloned.1.call-update) | async-done | bytes 5308432 | tf_op jit(solution)/shard_map/all_gather | solution.py:40
  503.9 102.0 %all-gather.8.cloned.1.call-done = bf16[1152,4608]{0,1:T(8,128)(2,1)} async-done(((bf16[1152,576]{0,1:T(8,128)(2,1)}), bf16[1152,4608]{0,1:T(8,128)(2,1)}) %all-gather.8.cloned.1.call-update) | async-done | bytes 10616848 | tf_op jit(solution)/shard_map/all_gather | solution.py:39
  605.9 13.1 %fusion.2 = bf16[1152,576]{0,1:T(8,128)(2,1)} fusion(bf16[4608,576]{0,1:T(8,128)(2,1)} %all-gather.10.cloned.1.call-done, bf16[1152,4608]{0,1:T(8,128)(2,1)} %all-gather.8.cloned.1.call-done, bf16[1152,576]{0,1:T(8,128)(2,1)} %convolution_convert_fusion), kind=kOutput, calls=%fused_computation.8 | convolution fusion | flops 6118612992 | bytes 18579456 | tf_op jit(solution)/shard_map/dot_general | solution.py:41
  618.9 0.0 all-gather.12.cloned.1.call-update
  619.0 83.1 %all-gather.14.cloned.1.call-done = bf16[4608,1024]{1,0:T(8,128)(2,1)} async-done(((bf16[1152,1024]{1,0:T(8,128)(2,1)}), bf16[4608,1024]{1,0:T(8,128)(2,1)}) %all-gather.14.cloned.1.call-update) | async-done | bytes 9437200 | tf_op jit(solution)/shard_map/all_gather | solution.py:46
  702.1 102.0 %all-gather.12.cloned.1.call-done = bf16[1152,4608]{0,1:T(8,128)(2,1)} async-done(((bf16[1152,576]{0,1:T(8,128)(2,1)}), bf16[1152,4608]{0,1:T(8,128)(2,1)}) %all-gather.12.cloned.1.call-update) | async-done | bytes 10616848 | tf_op jit(solution)/shard_map/all_gather | solution.py:43
  804.1 0.0 copy-done
  804.1 17.5 %fusion = f32[1152,1024]{1,0:T(8,128)} fusion(bf16[1152,4608]{0,1:T(8,128)(2,1)} %all-gather.12.cloned.1.call-done, bf16[4608,1024]{1,0:T(8,128)(2,1)} %all-gather.14.cloned.1.call-done, bf16[1152,1024]{1,0:T(8,128)(2,1)S(1)} %copy-done), kind=kOutput, calls=%fused_computation.2 | convolution fusion | flops 10876354560 | bytes 27131904 | tf_op jit(solution)/shard_map/dot_general | solution.py:44
Async XLA Ops:
  6.5 219.9 %all-gather.6.cloned.1.call-start = ((), (), s32[]{:S(2)}) async-start(), calls=%async_computation | async-start | bytes 21233664 | tf_op jit(solution)/shard_map/all_gather | solution.py:34
  58.0 365.0 %all-reduce.2.cloned.1.call-start = ((), (), s32[]{:S(2)}) async-start(), calls=%async_computation.1 | async-start | bytes 18874368 | tf_op jit(solution)/shard_map/psum | solution.py:16
  236.2 267.6 %all-gather.10.cloned.1.call-start = ((), (), s32[]{:S(2)}) async-start(), calls=%async_computation.3 | async-start | bytes 6635520 | tf_op jit(solution)/shard_map/all_gather | solution.py:40
  441.9 164.0 %all-gather.8.cloned.1.call-start = ((), (), s32[]{:S(2)}) async-start(), calls=%async_computation.2 | async-start | bytes 11943936 | tf_op jit(solution)/shard_map/all_gather | solution.py:39
  442.4 259.7 %all-gather.14.cloned.1.call-start = ((), (), s32[]{:S(2)}) async-start(), calls=%async_computation.5 | async-start | bytes 11796480 | tf_op jit(solution)/shard_map/all_gather | solution.py:46
  443.0 361.1 %copy-start = (bf16[1152,1024]{1,0:T(8,128)(2,1)S(1)}, bf16[1152,1024]{1,0:T(8,128)(2,1)}, u32[]{:S(2)}) copy-start(bf16[1152,1024]{1,0:T(8,128)(2,1)} %multiply_convert_fusion) | copy-start | bytes 7077892
  443.0 361.0 %all-gather.12.cloned.1.call-start = ((), (), s32[]{:S(2)}) async-start(), calls=%async_computation.4 | async-start | bytes 11943936 | tf_op jit(solution)/shard_map/all_gather | solution.py:43
Sparse Core Ops, SparseCore 0:
  58.2 168.2 all-gather.5
  236.4 186.5 all-reduce.1
  442.0 61.8 all-gather.9
  505.4 100.4 all-gather.7
  607.5 94.5 all-gather.13
  703.6 100.4 all-gather.11
where the time goes:
time: 829 us; the launch traced here: 828 us
  waiting for transfers between devices  704 us (85%)
  matrix products  49.4 us (6%)
  blocking collectives  42.2 us (5%)
  other arithmetic  18.3 us (2%)
  between operations  14.2 us (2%)
    psum x1, waiting for transfers between devices, from_root(): return lax.psum(jnp.where(mine, shard, jnp.zeros_like(shard)), axis)  187 us
    all_gather x1, waiting for transfers between devices, body(): row_panel = lax.all_gather(scaled, 'col', axis=1, tiled=True)  168 us
    all_gather x1, waiting for transfers between devices, body(): gram_panel = lax.all_gather(gram, 'col', axis=1, tiled=True)  102 us
    all_gather x1, waiting for transfers between devices, body(): poly_panel = lax.all_gather(poly, 'col', axis=1, tiled=True)  102 us
    all_gather x1, waiting for transfers between devices, body(): lax.all_gather(scaled, 'row', axis=0, tiled=True)  83.1 us
    all_gather x1, waiting for transfers between devices, body(): gram_columns = lax.all_gather(gram, 'row', axis=0, tiled=True)  60.6 us
    psum x1, blocking collectives, body(): norm_squares = lax.psum(partial_sum, ('row', 'col'))  42.2 us
    dot_general x1, matrix products, rows_product(): lax.dot_general(left, right, (((1,), (1,)), ((), ())), preferred_element_...  18.8 us
  transfers between devices with their start and end apart: 6, of which 6 were waited for; matrix products, arithmetic and copies ran while one was open for 2% of the time, Pallas kernels for 0%

commit v1 on v0

--- a/solution.py
+++ b/solution.py
@@ -31,7 +31,23 @@
     col_index = lax.axis_index("col")
     source_row = col_index // tile_ratio
     half_index = col_index % tile_ratio
-    row_panel = lax.all_gather(scaled, "col", axis=1, tiled=True)
+    size, index, rows = (lax.axis_size("col"), lax.axis_index("col"), scaled.shape[1])
+    route = [(i, (i + 1) % size) for i in range(size)]
+    backward = [(i, (i - 1) % size) for i in range(size)]
+    row_panel = jnp.zeros((*scaled.shape[:1], size * rows, *scaled.shape[1 + 1 :]), scaled.dtype)
+    row_panel = lax.dynamic_update_slice_in_dim(row_panel, scaled, index * rows, axis=1)
+    from_left = from_right = scaled
+    half = size // 2
+    for step in range(1, half + 1):
+        from_left = lax.ppermute(from_left, "col", route)
+        row_panel = lax.dynamic_update_slice_in_dim(
+            row_panel, from_left, (index - step) % size * rows, axis=1
+        )
+        if step < size - half:
+            from_right = lax.ppermute(from_right, "col", backward)
+            row_panel = lax.dynamic_update_slice_in_dim(
+                row_panel, from_right, (index + step) % size * rows, axis=1
+            )
     part_rows = row_panel.shape[0] // tile_ratio
     own_part = lax.dynamic_slice_in_dim(row_panel, half_index * part_rows, part_rows, 0)
     peer_rows = from_root(own_part, "row", source_row)

time: 829 us -> 861 us (1.039)
  local copies, waits for them, and re-layouts: 0.01 us -> 31.5 us
    all_gather x1 -> x0, waiting for transfers between devices: 168 us -> none  [body(): row_panel = lax.all_gather(scaled, 'col', axis=1, tiled=True)]
    ppermute x0 -> x7, waiting for transfers between devices: none -> 164 us  [the longest x4 164 us: body(): from_left = lax.ppermute(from_left, 'col', route)]
    dynamic_update_slice x0 -> x7, local copies, waits for them, and re-layouts: none -> 21.4 us  [the longest x4 11.6 us: body(): lax.dynamic_update_slice_in_dim(row_panel, from_left, (index - step) % si...]
  transfers between devices with their start and end apart: 6 -> 12, of which waited for: 6 -> 9; matrix products, arithmetic and copies ran while one was open for 2% -> 4% of each run, Pallas kernels for 0% -> 0%
where the time goes in v1:
time: 861 us
  waiting for transfers between devices  699 us (81%)
  matrix products  49.3 us (6%)
  blocking collectives  42.2 us (5%)
  local copies, waits for them, and re-layouts  31.5 us (4%)
  other arithmetic  16.3 us (2%)
  between operations  13.9 us (2%)
    psum x1, waiting for transfers between devices, from_root(): return lax.psum(jnp.where(mine, shard, jnp.zeros_like(shard)), axis)  187 us
    ppermute x4, waiting for transfers between devices, body(): from_left = lax.ppermute(from_left, 'col', route)  164 us
    all_gather x1, waiting for transfers between devices, body(): gram_panel = lax.all_gather(gram, 'col', axis=1, tiled=True)  102 us
    all_gather x1, waiting for transfers between devices, body(): poly_panel = lax.all_gather(poly, 'col', axis=1, tiled=True)  102 us
    all_gather x1, waiting for transfers between devices, body(): lax.all_gather(scaled, 'row', axis=0, tiled=True)  83.2 us
    all_gather x1, waiting for transfers between devices, body(): gram_columns = lax.all_gather(gram, 'row', axis=0, tiled=True)  60.4 us
    psum x1, blocking collectives, body(): norm_squares = lax.psum(partial_sum, ('row', 'col'))  42.2 us
    dot_general x1, matrix products, rows_product(): lax.dot_general(left, right, (((1,), (1,)), ((), ())), preferred_element_...  18.8 us
  transfers between devices with their start and end apart: 12, of which 9 were waited for; matrix products, arithmetic and copies ran while one was open for 4% of the time, Pallas kernels for 0%

profile of v1, /device:TPU:0, one launch (start us, length us, event | category | flops | bytes accessed | tf_op | source)
XLA Modules:
  0.0 860.9 jit_solution(5462717972462282817)
XLA Ops:
  6.5 0.0 all-reduce.2.cloned.1.call-start
  6.5 0.0 slice-start
  6.5 4.2 multiply_reduce_fusion
  10.8 42.2 %psum.14 = f32[]{:T(128)} all-reduce(f32[]{:T(128)} %multiply_reduce_fusion), channel_id=1, replica_groups=mesh['row'=4,'col'=8] {'row','col'}, use_global_device_ids=true, to_apply=%region_1.0 | all-reduce | flops 1 | bytes 8 | tf_op jit(solution)/shard_map/psum | solution.py:27
  53.7 0.0 slice-start.1
  53.7 7.3 broadcast_in_dim.6
  60.9 0.0 slice-done
  60.9 0.0 slice-done.1
  60.9 2.3 constant_dynamic-update-slice_fusion.7
  63.3 0.0 copy-start
  63.3 0.0 collective-permute-start
  63.3 3.5 collective-permute-start.1
  66.8 51.1 %collective-permute-done = bf16[1152,1024]{1,0:T(8,128)(2,1)S(1)} collective-permute-done((bf16[1152,1024]{1,0:T(8,128)(2,1)S(1)}, bf16[1152,1024]{1,0:T(8,128)(2,1)S(1)}, u32[]{:S(2)}, u32[]{:S(2)}) %collective-permute-start) | collective-permute-done | bytes 2359328 | tf_op jit(solution)/shard_map/ppermute | solution.py:42
  118.0 0.0 copy-start.2
  118.0 0.0 collective-permute-start.2
  118.0 0.0 collective-permute-done.1
  118.0 1.4 copy-done.2
  119.4 0.0 copy-start.3
  119.4 2.2 collective-permute-start.3
  121.6 50.7 %collective-permute-done.2 = bf16[1152,1024]{1,0:T(8,128)(2,1)S(1)} collective-permute-done((bf16[1152,1024]{1,0:T(8,128)(2,1)S(1)}, bf16[1152,1024]{1,0:T(8,128)(2,1)S(1)}, u32[]{:S(2)}, u32[]{:S(2)}) %collective-permute-start.2) | collective-permute-done | bytes 2359328 | tf_op jit(solution)/shard_map/ppermute | solution.py:42
  172.3 0.0 copy-done.3
  172.3 0.0 copy-start.4
  172.3 0.0 collective-permute-start.4
  172.3 0.0 collective-permute-done.3
  172.3 1.4 copy-done.4
  173.7 2.2 collective-permute-start.5
  175.9 49.6 %collective-permute-done.4 = bf16[1152,1024]{1,0:T(8,128)(2,1)} collective-permute-done((bf16[1152,1024]{1,0:T(8,128)(2,1)S(1)}, bf16[1152,1024]{1,0:T(8,128)(2,1)}, u32[]{:S(2)}, u32[]{:S(2)}) %collective-permute-start.4) | collective-permute-done | bytes 2359328 | tf_op jit(solution)/shard_map/ppermute | solution.py:42
  225.5 0.0 collective-permute-start.6
  225.5 0.0 copy-start.5
  225.5 3.4 constant_dynamic-update-slice_fusion.6
  228.9 3.3 constant_dynamic-update-slice_fusion.5
  232.2 0.0 copy-done.5
  232.2 1.6 constant_dynamic-update-slice_fusion.4
  233.8 3.3 constant_dynamic-update-slice_fusion.3
  237.1 0.0 copy-done
  237.1 3.3 constant_dynamic-update-slice_fusion.2
  240.4 0.0 collective-permute-done.5
  240.4 3.3 constant_dynamic-update-slice_fusion.1
  243.6 12.2 %collective-permute-done.6 = bf16[1152,1024]{1,0:T(8,128)(2,1)} collective-permute-done((bf16[1152,1024]{1,0:T(8,128)(2,1)}, bf16[1152,1024]{1,0:T(8,128)(2,1)}, u32[]{:S(2)}, u32[]{:S(2)}) %collective-permute-start.6) | collective-permute-done | bytes 2359328 | tf_op jit(solution)/shard_map/ppermute | solution.py:42
  255.8 3.3 constant_dynamic-update-slice_fusion
  259.1 9.8 %dynamic-slice_select_fusion = bf16[576,8192]{1,0:T(8,128)(2,1)} fusion(bf16[1152,8192]{1,0:T(8,128)(2,1)} %constant_dynamic-update-slice_fusion, s32[]{:T(128)S(6)} %select_n.92, pred[]{:T(512)S(6)} %eq.12), kind=kLoop, calls=%fused_computation | loop fusion | flops 4718592 | bytes 18874372 | tf_op jit(solution)/shard_map/jit(_where)/select_n | solution.py:16
  268.9 0.0 all-reduce.2.cloned.1.call-update
  268.9 0.0 all-gather.7.cloned.1.call-start
  269.0 186.8 %all-reduce.2.cloned.1.call-done = bf16[576,8192]{1,0:T(8,128)(2,1)} async-done(((bf16[576,8192]{1,0:T(8,128)(2,1)}), bf16[576,8192]{1,0:T(8,128)(2,1)}) %all-reduce.2.cloned.1.call-update) | async-done | bytes 9437200 | tf_op jit(solution)/shard_map/psum | solution.py:16
  455.7 18.8 %convolution_convert_fusion = bf16[1152,576]{0,1:T(8,128)(2,1)} fusion(bf16[1152,8192]{1,0:T(8,128)(2,1)} %constant_dynamic-update-slice_fusion, bf16[576,8192]{1,0:T(8,128)(2,1)} %all-reduce.2.cloned.1.call-done), kind=kOutput, calls=%fused_computation.6 | convolution fusion | flops 10872299520 | bytes 29638656 | tf_op jit(solution)/shard_map/dot_general | solution.py:20
  474.5 0.0 all-gather.7.cloned.1.call-update
  474.6 0.0 all-gather.5.cloned.1.call-start
  474.6 0.7 all-gather.5.cloned.1.call-update
  475.3 0.0 all-gather.11.cloned.1.call-start
  475.3 0.5 all-gather.11.cloned.1.call-update
  475.9 0.0 copy-start.1
  475.9 0.2 all-gather.9.cloned.1.call-start
  476.1 60.4 %all-gather.7.cloned.1.call-done = bf16[4608,576]{0,1:T(8,128)(2,1)} async-done(((bf16[1152,576]{0,1:T(8,128)(2,1)}), bf16[4608,576]{0,1:T(8,128)(2,1)}) %all-gather.7.cloned.1.call-update) | async-done | bytes 5308432 | tf_op jit(solution)/shard_map/all_gather | solution.py:56
  536.6 102.1 %all-gather.5.cloned.1.call-done = bf16[1152,4608]{0,1:T(8,128)(2,1)} async-done(((bf16[1152,576]{0,1:T(8,128)(2,1)}), bf16[1152,4608]{0,1:T(8,128)(2,1)}) %all-gather.5.cloned.1.call-update) | async-done | bytes 10616848 | tf_op jit(solution)/shard_map/all_gather | solution.py:55
  638.7 13.1 %add_convert_fusion = bf16[1152,576]{0,1:T(8,128)(2,1)} fusion(bf16[1152,576]{0,1:T(8,128)(2,1)} %convolution_convert_fusion, bf16[4608,576]{0,1:T(8,128)(2,1)} %all-gather.7.cloned.1.call-done, bf16[1152,4608]{0,1:T(8,128)(2,1)} %all-gather.5.cloned.1.call-done), kind=kOutput, calls=%fused_computation.7 | convolution fusion | flops 6118612992 | bytes 18579456 | tf_op jit(solution)/shard_map/dot_general | solution.py:57
  651.8 0.0 all-gather.9.cloned.1.call-update
  651.8 83.2 %all-gather.11.cloned.1.call-done = bf16[4608,1024]{1,0:T(8,128)(2,1)} async-done(((bf16[1152,1024]{1,0:T(8,128)(2,1)}), bf16[4608,1024]{1,0:T(8,128)(2,1)}) %all-gather.11.cloned.1.call-update) | async-done | bytes 9437200 | tf_op jit(solution)/shard_map/all_gather | solution.py:62
  735.0 102.0 %all-gather.9.cloned.1.call-done = bf16[1152,4608]{0,1:T(8,128)(2,1)} async-done(((bf16[1152,576]{0,1:T(8,128)(2,1)}), bf16[1152,4608]{0,1:T(8,128)(2,1)}) %all-gather.9.cloned.1.call-update) | async-done | bytes 10616848 | tf_op jit(solution)/shard_map/all_gather | solution.py:59
  836.9 0.0 copy-done.1
  836.9 17.5 %fusion = f32[1152,1024]{1,0:T(8,128)} fusion(bf16[1152,4608]{0,1:T(8,128)(2,1)} %all-gather.9.cloned.1.call-done, bf16[4608,1024]{1,0:T(8,128)(2,1)} %all-gather.11.cloned.1.call-done, bf16[1152,1024]{1,0:T(8,128)(2,1)S(1)} %copy-done.1), kind=kOutput, calls=%fused_computation.2 | convolution fusion | flops 10876354560 | bytes 27131904 | tf_op jit(solution)/shard_map/dot_general | solution.py:60
  (1 shorter events, 0.0 us)
Async XLA Ops:
  6.5 449.2 %all-reduce.2.cloned.1.call-start = ((), (), s32[]{:S(2)}) async-start(), calls=%async_computation | async-start | bytes 18874368 | tf_op jit(solution)/shard_map/psum | solution.py:16
  6.5 54.4 %slice-start = ((s8[4718592]{0:T(1024)(128)(4,1)}), s8[524288]{0:T(1024)(128)(4,1)S(1)}, s32[]{:S(2)}) async-start(s8[4718592]{0:T(1024)(128)(4,1)} %bitcast.6), calls=%async_computation.5 | async-start | bytes 1048576
  53.7 7.3 slice-start.1
  63.3 173.8 %copy-start = (bf16[1152,1024]{1,0:T(8,128)(2,1)}, bf16[1152,1024]{1,0:T(8,128)(2,1)S(1)}, u32[]{:S(2)}) copy-start(bf16[1152,1024]{1,0:T(8,128)(2,1)S(1)} %get-tuple-element.6) | copy-start | bytes 7077892
  63.3 54.7 %collective-permute-start = (bf16[1152,1024]{1,0:T(8,128)(2,1)S(1)}, bf16[1152,1024]{1,0:T(8,128)(2,1)S(1)}, u32[]{:S(2)}, u32[]{:S(2)}) collective-permute-start(bf16[1152,1024]{1,0:T(8,128)(2,1)S(1)} %get-tuple-element.6), channel_id=1, source_target_pairs={{0,1},{1,2},{2,3},{3,4},{4,5},{5,6},{6,7},{7,0},{8,9},{9,10},{10,1... | collective-permute-start | bytes 7077896 | tf_op jit(solution)/shard_map/ppermute | solution.py:42
  63.3 54.7 %collective-permute-start.1 = (bf16[1152,1024]{1,0:T(8,128)(2,1)S(1)}, bf16[1152,1024]{1,0:T(8,128)(2,1)S(1)}, u32[]{:S(2)}, u32[]{:S(2)}) collective-permute-start(bf16[1152,1024]{1,0:T(8,128)(2,1)S(1)} %get-tuple-element.6), channel_id=1, source_target_pairs={{0,7},{1,0},{2,1},{3,2},{4,3},{5,4},{6,5},{7,6},{8,15},{9,8},{10,9... | collective-permute-start | bytes 7077896 | tf_op jit(solution)/shard_map/ppermute | solution.py:47
  118.0 1.4 copy-start.2
  118.0 54.3 %collective-permute-start.2 = (bf16[1152,1024]{1,0:T(8,128)(2,1)S(1)}, bf16[1152,1024]{1,0:T(8,128)(2,1)S(1)}, u32[]{:S(2)}, u32[]{:S(2)}) collective-permute-start(bf16[1152,1024]{1,0:T(8,128)(2,1)S(1)} %collective-permute-done), channel_id=1, source_target_pairs={{0,1},{1,2},{2,3},{3,4},{4,5},{5,6},{6,7},{7,0},{8,9},{9,10},{10,1... | collective-permute-start | bytes 7077896 | tf_op jit(solution)/shard_map/ppermute | solution.py:42
  119.4 52.9 %copy-start.3 = (bf16[1152,1024]{1,0:T(8,128)(2,1)}, bf16[1152,1024]{1,0:T(8,128)(2,1)S(1)}, u32[]{:S(2)}) copy-start(bf16[1152,1024]{1,0:T(8,128)(2,1)S(1)} %collective-permute-done.1) | copy-start | bytes 7077892
  119.4 53.0 %collective-permute-start.3 = (bf16[1152,1024]{1,0:T(8,128)(2,1)S(1)}, bf16[1152,1024]{1,0:T(8,128)(2,1)}, u32[]{:S(2)}, u32[]{:S(2)}) collective-permute-start(bf16[1152,1024]{1,0:T(8,128)(2,1)S(1)} %collective-permute-done.1), channel_id=1, source_target_pairs={{0,7},{1,0},{2,1},{3,2},{4,3},{5,4},{6,5},{7,6},{8,15},{9,8},{10,9... | collective-permute-start | bytes 7077896 | tf_op jit(solution)/shard_map/ppermute | solution.py:47
  172.3 1.4 copy-start.4
  172.3 53.2 %collective-permute-start.4 = (bf16[1152,1024]{1,0:T(8,128)(2,1)S(1)}, bf16[1152,1024]{1,0:T(8,128)(2,1)}, u32[]{:S(2)}, u32[]{:S(2)}) collective-permute-start(bf16[1152,1024]{1,0:T(8,128)(2,1)S(1)} %collective-permute-done.2), channel_id=1, source_target_pairs={{0,1},{1,2},{2,3},{3,4},{4,5},{5,6},{6,7},{7,0},{8,9},{9,10},{10,1... | collective-permute-start | bytes 7077896 | tf_op jit(solution)/shard_map/ppermute | solution.py:42
  173.7 66.7 %collective-permute-start.5 = (bf16[1152,1024]{1,0:T(8,128)(2,1)}, bf16[1152,1024]{1,0:T(8,128)(2,1)}, u32[]{:S(2)}, u32[]{:S(2)}) collective-permute-start(bf16[1152,1024]{1,0:T(8,128)(2,1)} %collective-permute-done.3), channel_id=1, source_target_pairs={{0,7},{1,0},{2,1},{3,2},{4,3},{5,4},{6,5},{7,6},{8,15},{9,8},{10,9... | collective-permute-start | bytes 7077896 | tf_op jit(solution)/shard_map/ppermute | solution.py:47
  225.5 30.4 %collective-permute-start.6 = (bf16[1152,1024]{1,0:T(8,128)(2,1)}, bf16[1152,1024]{1,0:T(8,128)(2,1)}, u32[]{:S(2)}, u32[]{:S(2)}) collective-permute-start(bf16[1152,1024]{1,0:T(8,128)(2,1)} %collective-permute-done.4), channel_id=1, source_target_pairs={{0,1},{1,2},{2,3},{3,4},{4,5},{5,6},{6,7},{7,0},{8,9},{9,10},{10,1... | collective-permute-start | bytes 7077896 | tf_op jit(solution)/shard_map/ppermute | solution.py:42
  225.5 6.8 copy-start.5
  268.9 267.6 %all-gather.7.cloned.1.call-start = ((), (), s32[]{:S(2)}) async-start(), calls=%async_computation.2 | async-start | bytes 6635520 | tf_op jit(solution)/shard_map/all_gather | solution.py:56
  474.6 164.1 %all-gather.5.cloned.1.call-start = ((), (), s32[]{:S(2)}) async-start(), calls=%async_computation.1 | async-start | bytes 11943936 | tf_op jit(solution)/shard_map/all_gather | solution.py:55
  475.3 259.7 %all-gather.11.cloned.1.call-start = ((), (), s32[]{:S(2)}) async-start(), calls=%async_computation.4 | async-start | bytes 11796480 | tf_op jit(solution)/shard_map/all_gather | solution.py:62
  475.9 361.1 %copy-start.1 = (bf16[1152,1024]{1,0:T(8,128)(2,1)S(1)}, bf16[1152,1024]{1,0:T(8,128)(2,1)}, u32[]{:S(2)}) copy-start(bf16[1152,1024]{1,0:T(8,128)(2,1)} %copy-done) | copy-start | bytes 7077892
  475.9 361.1 %all-gather.9.cloned.1.call-start = ((), (), s32[]{:S(2)}) async-start(), calls=%async_computation.3 | async-start | bytes 11943936 | tf_op jit(solution)/shard_map/all_gather | solution.py:59
Sparse Core Ops, SparseCore 0:
  269.0 186.6 all-reduce.1
  474.7 61.8 all-gather.6
  538.2 100.4 all-gather.4
  640.4 94.5 all-gather.10
  736.4 100.4 all-gather.8
